TPU v7x, 128 devices: a whole 4x4x4 slice. The times are simulated.
128 devices in a mesh: item: 4 (over x), row: 16 (over z, y), col: 2 (over core).
Axes of the slice: x: 4, y: 4, z: 4, core: 2. Of those that a mesh axis runs over, the one named last changes fastest.
Arguments:
- img_hidden: bfloat16 [32, 1024, 3072], P('item', ('row', 'col')), parts along dimension 0, may hold values from -1.796875 to 1.796875
- text_hidden: bfloat16 [32, 512, 3072], P('item', ('row', 'col')), parts along dimension 0, may hold values from -1.796875 to 1.796875
- latent: float32 [32, 1024, 64], P('item', ('row', 'col')), parts along dimension 0, may hold values from -6 to 6
- text_len: int32 [32], P('item'), parts along dimension 0, may hold values from 1 to 512, as said below
- block_keep: int32 [32, 16], P('item'), parts along dimension 0, may hold values 0 or 1
- img_pos: int32 [1024, 3], P(('row', 'col')), may hold values from 0 to 62, as said below
- modulation: float32 [32, 5, 3072], P('item'), parts along dimension 0, may hold values from -4 to 4
- qk_gain: float32 [2, 128], replicated, may hold values from 0.7 to 7
- w_qkv: bfloat16 [3072, 3, 1536], P(None, None, 'col'), may hold values from -0.109375 to 0.109375
- w_out: bfloat16 [1536, 3072], P('col'), may hold values from -0.25 to 0.25
- w_final: bfloat16 [3072, 64], replicated, may hold values from -0.109375 to 0.109375
Outputs:
- img_out: bfloat16 [32, 1024, 3072], P('item', ('row', 'col')), parts along dimension 0
- text_out: bfloat16 [32, 512, 3072], P('item', ('row', 'col')), parts along dimension 0
- latent_next: float32 [32, 1024, 64], P('item', ('row', 'col')), parts along dimension 0
There are 4 independent parts, one for each index of `item`. A program takes and returns all parts, laid end to end along the dimension named above; an argument that names none is the same for every part. Nothing has to cross between parts.
Inputs may be any that keep to these rules, and one draw needn't show every extreme that they name: `text_len`: at least one sample of every request uses all 512 text slots. `img_pos`: image token i, in image row r = i // 32 and column q = i % 32, has ids (c_i, a_r + r, b_q + q), where every token has its own frame id c_i of 0 to 3, every image row its own offset a_r and every image column its own offset b_q, each of 0 to 31.
All inputs are finite; a program needn't handle non-finite values.
Results may differ from a plain program's by a relative error of at most 0.015.
The roundings to bfloat16 on the way count: a program that leaves them out, or rounds other values in their place, can miss the bound.
Values may be sent and summed in bfloat16 or wider, within the bound.
No kernel may reach another device: no remote copies, remote signals or barrier semaphores. Data moves between devices by JAX's collectives and lax.ppermute only.
A program may use at most 256 MiB of HBM per device.

v0:
```python
import jax
import jax.numpy as jnp
import numpy as np
from jax import lax
from jax.sharding import PartitionSpec as P

KBLK = 64
eps_norm = 1e-06
theta_base = 10000.0
step_size = -0.25


def layer_norm(values):
    center = values - jnp.mean(values, axis=-1, keepdims=True)
    return center * lax.rsqrt(jnp.mean(center * center, axis=-1, keepdims=True) + eps_norm)


def modulate(hidden, shift, scale):
    return ((1.0 + scale) * layer_norm(hidden.astype(jnp.float32)) + shift).astype(jnp.bfloat16)


def rope_tables(head_dim):
    half = head_dim // 2
    first = head_dim // 16
    second = (half - first) // 2
    counts = [first, second, half - first - second]
    tables = []
    for axis_id in range(3):
        pieces = []
        for other in range(3):
            if other == axis_id:
                pieces.append(theta_base ** (-np.arange(counts[other]) / counts[other]))
            else:
                pieces.append(np.zeros(counts[other]))
        tables.append(np.concatenate(pieces).astype(np.float32))
    return tables


def angles_of(positions, head_dim):
    tables = rope_tables(head_dim)
    angle = positions[:, 0:1] * jnp.asarray(tables[0]) + positions[:, 1:2] * jnp.asarray(tables[1])
    angle = angle + positions[:, 2:3] * jnp.asarray(tables[2])
    return (jnp.cos(angle), jnp.sin(angle))


def rotate(values, cosine, sine):
    half = values.shape[-1] // 2
    first_half = values[..., :half]
    second_half = values[..., half:]
    cos_rows = cosine[:, None, :]
    sin_rows = sine[:, None, :]
    return jnp.concatenate(
        [
            first_half * cos_rows - second_half * sin_rows,
            second_half * cos_rows + first_half * sin_rows,
        ],
        axis=-1,
    )


def rms_gain(values, gain):
    return values * lax.rsqrt(jnp.mean(values * values, axis=-1, keepdims=True) + eps_norm) * gain


def valid_keys(text_len, block_keep, count, text_rows, img_rows):
    group = text_rows + img_rows
    index = jnp.arange(count, dtype=jnp.int32)
    device = index // group
    local = index % group
    is_text = local < text_rows
    text_index = device * text_rows + local
    img_index = device * img_rows + jnp.maximum(local - text_rows, 0)
    text_ok = text_index[None, :] < text_len[:, None]
    onehot = (
        (img_index // KBLK)[:, None] == jnp.arange(block_keep.shape[1], dtype=jnp.int32)[None, :]
    ).astype(jnp.int32)
    img_ok = jnp.sum(block_keep[:, None, :] * onehot[None], axis=-1) > 0
    return jnp.where(is_text[None, :], text_ok, img_ok)


def absorb(state, piece, valid, query):
    top, total, summed = state
    key_piece, value_piece = piece
    samples = key_piece.shape[0]
    count = key_piece.shape[1]
    heads = query.shape[2]
    head_dim = query.shape[3]
    key_split = key_piece.reshape(samples, count, heads, head_dim)
    value_split = value_piece.reshape(samples, count, heads, head_dim)
    scores = jnp.einsum(
        "sqhd,skhd->shqk", query, key_split, preferred_element_type=jnp.float32
    ) * head_dim ** (-0.5)
    scores = jnp.where(valid[:, None, None, :], scores, -jnp.inf)
    new_top = jnp.maximum(top, jnp.max(scores, axis=-1))
    weights = jnp.exp(scores - new_top[..., None])
    factor = jnp.exp(top - new_top)
    total = total * factor + jnp.sum(weights, axis=-1)
    summed = summed * factor[..., None] + jnp.einsum(
        "shqk,skhd->shqd",
        weights.astype(jnp.bfloat16),
        value_split,
        preferred_element_type=jnp.float32,
    )
    return (new_top, total, summed)


def per_device(
    img_hidden,
    text_hidden,
    latent,
    text_len,
    block_keep,
    img_pos,
    modulation,
    qk_gain,
    w_qkv,
    w_out,
    w_final,
):
    samples = img_hidden.shape[0]
    width = img_hidden.shape[2]
    head_dim = qk_gain.shape[1]
    local_inner = w_out.shape[0]
    local_heads = local_inner // head_dim
    mod_rows = modulation[:, :, None, :]
    text_norm = modulate(text_hidden, mod_rows[:, 0], mod_rows[:, 1])
    img_norm = modulate(img_hidden, mod_rows[:, 0], mod_rows[:, 1])
    text_group, img_group, pos_group = (
        lax.all_gather(text_norm, "col", axis=1, tiled=True),
        lax.all_gather(img_norm, "col", axis=1, tiled=True),
        lax.all_gather(img_pos.astype(jnp.bfloat16), "col", axis=0, tiled=True),
    )
    text_rows = text_group.shape[1]
    img_rows = img_group.shape[1]
    group = text_rows + img_rows
    joined = jnp.concatenate([text_group, img_group], axis=1)
    mixed = jnp.dot(
        joined.reshape(samples * group, width),
        w_qkv.reshape(width, 3 * local_inner),
        preferred_element_type=jnp.float32,
    )
    mixed = mixed.reshape(samples, group, 3, local_heads, head_dim)
    positions = jnp.concatenate(
        [jnp.zeros((text_rows, 3), jnp.float32), pos_group.astype(jnp.float32)], axis=0
    )
    cosine, sine = angles_of(positions, head_dim)
    query = rotate(rms_gain(mixed[:, :, 0], qk_gain[0]), cosine, sine).astype(jnp.bfloat16)
    keys = (
        rotate(rms_gain(mixed[:, :, 1], qk_gain[1]), cosine, sine)
        .astype(jnp.bfloat16)
        .reshape(samples, group, local_inner)
    )
    values = mixed[:, :, 2].astype(jnp.bfloat16).reshape(samples, group, local_inner)
    start_state = (
        jnp.full((samples, local_heads, group), -1e30, jnp.float32),
        jnp.zeros((samples, local_heads, group), jnp.float32),
        jnp.zeros((samples, local_heads, group, head_dim), jnp.float32),
    )
    piece = (
        lax.all_gather(keys, "row", axis=1, tiled=True),
        lax.all_gather(values, "row", axis=1, tiled=True),
    )
    count = piece[0].shape[1]
    valid = valid_keys(text_len, block_keep, count, text_rows, img_rows)
    top, total, summed = absorb(start_state, piece, valid, query)
    attention = jnp.transpose(summed / total[..., None], (0, 2, 1, 3)).astype(jnp.bfloat16)
    attention = attention.reshape(samples, group, local_inner)
    partial_sum = jnp.dot(
        attention.reshape(samples * group, local_inner), w_out, preferred_element_type=jnp.float32
    )
    partial_sum = partial_sum.reshape(samples, group, width)
    text_sum, img_sum = (
        lax.psum_scatter(
            partial_sum[:, :text_rows].astype(jnp.bfloat16), "col", scatter_dimension=1, tiled=True
        ).astype(jnp.float32),
        lax.psum_scatter(
            partial_sum[:, text_rows:].astype(jnp.bfloat16), "col", scatter_dimension=1, tiled=True
        ).astype(jnp.float32),
    )
    text_out = (text_hidden.astype(jnp.float32) + mod_rows[:, 2] * text_sum).astype(jnp.bfloat16)
    img_out = (img_hidden.astype(jnp.float32) + mod_rows[:, 2] * img_sum).astype(jnp.bfloat16)
    final = modulate(img_out, mod_rows[:, 3], mod_rows[:, 4])
    velocity = jnp.dot(
        final.reshape(samples * img_hidden.shape[1], width),
        w_final,
        preferred_element_type=jnp.float32,
    )
    velocity = velocity.reshape(samples, img_hidden.shape[1], w_final.shape[1])
    return (img_out, text_out, latent + step_size * velocity)


def solution(mesh):
    placed = (
        P("item", ("row", "col"), None),
        P("item", ("row", "col"), None),
        P("item", ("row", "col"), None),
        P("item"),
        P("item", None),
        P(("row", "col"), None),
        P("item", None, None),
        P(),
        P(None, None, "col"),
        P("col", None),
        P(),
    )
    return jax.shard_map(
        per_device,
        mesh=mesh,
        in_specs=placed,
        out_specs=(
            P("item", ("row", "col"), None),
            P("item", ("row", "col"), None),
            P("item", ("row", "col"), None),
        ),
        check_vma=False,
    )
```

profile of v0, /device:TPU:1, one launch (start us, length us, event | category | flops | bytes accessed | tf_op | source)
XLA Modules:
  0.0 409.7 jit_solution(13633441374526397716)
XLA Ops:
  13.6 2.0 fusion.20
  15.7 18.7 %copy.38 = bf16[3072,3,768]{0,2,1:T(8,128)(2,1)} copy(bf16[3072,3,768]{2,0,1:T(8,128)(2,1)} %param.22) | data formatting | bytes 28311552 | tf_op args[8]
  34.4 3.0 all-gather
  37.8 9.6 %all-gather.8.cloned.1.call-done = bf16[8,64,3072]{2,1,0:T(8,128)(2,1)} async-done(((bf16[8,32,3072]{2,1,0:T(8,128)(2,1)}), bf16[8,64,3072]{2,1,0:T(8,128)(2,1)}) %all-gather.8.cloned.1.call-update) | async-done | bytes 3145744 | tf_op jit(solution)/shard_map/all_gather | solution.py:130
  47.4 14.7 %fusion.9 = f32[8,96,3,6,128]{4,1,3,2,0:T(8,128)S(1)} fusion(bf16[3,6,128,3072,1]{3,2,1,0,4:T(8,128)(2,1)} %bitcast.90, bf16[8,64,3072]{2,1,0:T(8,128)(2,1)} %all-gather.8.cloned.1.call-done, bf16[8,32,3072]{2,1,0:T(8,128)(2,1)} %all-gather.6.cloned.1.call-done), kind=kOutput, calls=%fused_computation.15 | convolution fusion | flops 10881073152 | bytes 25952256 | tf_op jit(solution)/shard_map/dot_general | solution.py:137
  62.1 1.7 multiply_reduce_fusion.1
  65.4 2.8 subtract_convert_fusion.1
  69.9 1.8 slice.129
  71.7 1.7 copy.44
  73.4 3.8 convert_element_type.70
  77.9 115.2 %all-gather.10.cloned.1.call-done = bf16[8,1536,768]{2,1,0:T(8,128)(2,1)} async-done(((bf16[8,96,768]{2,1,0:T(8,128)(2,1)}), bf16[8,1536,768]{2,1,0:T(8,128)(2,1)}) %all-gather.10.cloned.1.call-update) | async-done | bytes 18874384 | tf_op jit(solution)/shard_map/all_gather | solution.py:160
  193.0 24.9 %copy.42 = bf16[8,1536,768]{1,2,0:T(8,128)(2,1)} copy(bf16[8,1536,768]{2,1,0:T(8,128)(2,1)} %all-gather.10.cloned.1.call-done) | data formatting | bytes 37748736 | tf_op jit(solution)/shard_map/all_gather | solution.py:160
  217.9 16.8 %fusion = (f32[8,6,96]{2,1,0:T(8,128)S(1)}, f32[8,6,96,1536]{3,2,1,0:T(8,128)}) fusion(pred[8,1536]{1,0:T(8,128)(4,1)S(1)} %compare_select_fusion, bf16[8,1536,6,128]{1,3,2,0:T(8,128)(2,1)} %bitcast.88, bf16[8,96,6,64]{3,1,2,0:T(8,128)(2,1)} %get-tuple-element.10, bf16[8,96,6,64]{3,1,2,0:T(8,128)(2,1)} %get-tuple-element.9), kind=kOutput, calls=%fused_computation.2 | convolution fusion | flops 1835527680 | bytes 48396288 | tf_op jit(solution)/shard_map/sqhd,skhd->shqk/dot_general | solution.py:90
  234.7 11.8 %fusion.1 = f32[8,6,96]{2,1,0:T(8,128)S(1)} fusion(f32[8,6,96,1536]{3,2,1,0:T(8,128)} %get-tuple-element.30, f32[8,6,96]{2,1,0:T(8,128)S(1)} %get-tuple-element.21, pred[8,1536]{1,0:T(8,128)(4,1)S(1)} %compare_select_fusion), kind=kLoop, calls=%fused_computation.3 | loop fusion | flops 28306944 | bytes 28360704 | tf_op jit(solution)/shard_map/reduce_sum | solution.py:97
  246.5 70.3 %all-gather.12.cloned.1.call-done = bf16[8,1536,768]{2,1,0:T(8,128)(2,1)} async-done(((bf16[8,96,768]{2,1,0:T(8,128)(2,1)}), bf16[8,1536,768]{2,1,0:T(8,128)(2,1)}) %all-gather.12.cloned.1.call-update) | async-done | bytes 18874384 | tf_op jit(solution)/shard_map/all_gather | solution.py:161
  316.8 24.7 %copy.45 = bf16[8,1536,768]{1,2,0:T(8,128)(2,1)} copy(bf16[8,1536,768]{2,1,0:T(8,128)(2,1)} %all-gather.12.cloned.1.call-done) | data formatting | bytes 37748736 | tf_op jit(solution)/shard_map/all_gather | solution.py:161
  341.5 18.1 %fusion.39 = bf16[8,6,12,8,128]{4,3,2,1,0:T(8,128)(2,1)} fusion(bf16[8,1536,6,128]{1,3,2,0:T(8,128)(2,1)} %bitcast.89, f32[8,6,96,1536]{3,2,1,0:T(8,128)} %get-tuple-element.30, f32[8,6,96]{2,1,0:T(8,128)S(1)} %get-tuple-element.21, pred[8,1536]{1,0:T(8,128)(4,1)S(1)} %compare_select_fusion, f32[8,96,6]{1,2,0:T(8,128)S(1)} %bitcast_add_fusion.1, ...), kind=kOutput, calls=%fused_computation.59 | convolution fusion | flops 1842020352 | bytes 48433152 | tf_op jit(solution)/shard_map/shqk,skhd->shqd/dot_general | solution.py:98
  359.6 6.5 %convolution_convert_fusion = bf16[8,96,3072]{2,1,0:T(8,128)(2,1)S(1)} fusion(bf16[768,3072]{1,0:T(8,128)(2,1)} %param.23, bf16[8,6,12,8,128]{4,3,2,1,0:T(8,128)(2,1)} %fusion.39), kind=kOutput, calls=%fused_computation.10 | convolution fusion | flops 3626237952 | bytes 10616832 | tf_op jit(solution)/shard_map/dot_general | solution.py:168
  366.1 2.1 copy-done.5
  369.8 3.8 slice.92
  373.6 7.9 %reduce-scatter.5.cloned.1.call-done = bf16[8,16,3072]{2,1,0:T(8,128)(2,1)} async-done(((bf16[8,32,3072]{2,1,0:T(8,128)(2,1)}), bf16[8,16,3072]{2,1,0:T(8,128)(2,1)}) %reduce-scatter.5.cloned.1.call-update) | async-done | bytes 786448 | tf_op jit(solution)/shard_map/reduce_scatter | solution.py:173
  381.4 2.2 fusion.36
  383.7 15.0 %reduce-scatter.3.cloned.1.call-done = bf16[8,32,3072]{2,1,0:T(8,128)(2,1)} async-done(((bf16[8,64,3072]{2,1,0:T(8,128)(2,1)}), bf16[8,32,3072]{2,1,0:T(8,128)(2,1)}) %reduce-scatter.3.cloned.1.call-update) | async-done | bytes 1572880 | tf_op jit(solution)/shard_map/reduce_scatter | solution.py:176
  398.7 2.1 convert_reduce_fusion.1
  (73 shorter events, 14.4 us)
Async XLA Ops:
  7.2 394.3 %copy-start = (bf16[3072,64]{0,1:T(8,128)(2,1)S(1)}, bf16[3072,64]{0,1:T(8,128)(2,1)}, u32[]{:S(2)}) copy-start(bf16[3072,64]{0,1:T(8,128)(2,1)} %param.24) | copy-start | bytes 1179652
  7.2 4.1 %copy-start.3 = (bf16[8,16,3072]{2,1,0:T(8,128)(2,1)S(1)}, bf16[8,16,3072]{2,1,0:T(8,128)(2,1)}, u32[]{:S(2)}) copy-start(bf16[8,16,3072]{2,1,0:T(8,128)(2,1)} %param.15) | copy-start | bytes 2359300
  7.2 30.6 %all-gather.6.cloned.1.call-start = ((), (), s32[]{:S(2)}) async-start(), calls=%async_computation.2 | async-start | bytes 2359296 | tf_op jit(solution)/shard_map/all_gather | solution.py:129
  7.2 5.5 %copy-start.1 = (bf16[8,32,3072]{2,1,0:T(8,128)(2,1)S(1)}, bf16[8,32,3072]{2,1,0:T(8,128)(2,1)}, u32[]{:S(2)}) copy-start(bf16[8,32,3072]{2,1,0:T(8,128)(2,1)} %param.14) | copy-start | bytes 4718596
  12.7 34.7 %all-gather.8.cloned.1.call-start = ((), (), s32[]{:S(2)}) async-start(), calls=%async_computation.3 | async-start | bytes 4718592 | tf_op jit(solution)/shard_map/all_gather | solution.py:130
  15.6 18.8 %copy-start.7 = (s32[32,3]{0,1:T(4,128)S(1)}, s32[32,3]{0,1:T(4,128)}, u32[]{:S(2)}) copy-start(s32[32,3]{0,1:T(4,128)} %param.19) | copy-start | bytes 1156
  15.6 21.9 %copy-start.8 = (f32[2,128]{1,0:T(2,128)S(1)}, f32[2,128]{1,0:T(2,128)}, u32[]{:S(2)}) copy-start(f32[2,128]{1,0:T(2,128)} %param.21) | copy-start | bytes 3076
  15.6 21.9 %copy-start.10 = (f32[64]{0:T(128)S(1)}, f32[64]{0:T(128)}, u32[]{:S(2)}) copy-start(f32[64]{0:T(128)} %constant.80.clone) | copy-start | bytes 772
  15.6 21.9 %copy-start.11 = (f32[64]{0:T(128)S(1)}, f32[64]{0:T(128)}, u32[]{:S(2)}) copy-start(f32[64]{0:T(128)} %constant.81.clone) | copy-start | bytes 772
  15.6 21.9 %copy-start.12 = (f32[64]{0:T(128)S(1)}, f32[64]{0:T(128)}, u32[]{:S(2)}) copy-start(f32[64]{0:T(128)} %constant.82.clone) | copy-start | bytes 772
  15.6 177.4 %all-gather.10.cloned.1.call-start = ((), (), s32[]{:S(2)}) async-start(), calls=%async_computation.4 | async-start | bytes 20054016 | tf_op jit(solution)/shard_map/all_gather | solution.py:160
  62.1 3.3 copy-start.2
  69.8 247.0 %all-gather.12.cloned.1.call-start = ((), (), s32[]{:S(2)}) async-start(), calls=%async_computation.5 | async-start | bytes 20054016 | tf_op jit(solution)/shard_map/all_gather | solution.py:161
  73.4 4.2 %copy-start.6 = (s32[8,16]{1,0:T(8,128)S(1)}, s32[8,16]{1,0:T(8,128)}, u32[]{:S(2)}) copy-start(s32[8,16]{1,0:T(8,128)} %param.18) | copy-start | bytes 1540
  73.4 4.4 %copy-start.9 = (s32[8]{0:T(128)S(1)}, s32[8]{0:T(128)}, u32[]{:S(2)}) copy-start(s32[8]{0:T(128)} %param.17) | copy-start | bytes 100
  77.2 304.2 %reduce-scatter.5.cloned.1.call-start = ((), (), s32[]{:S(2)}) async-start(), calls=%async_computation.7 | async-start | bytes 2359296 | tf_op jit(solution)/shard_map/reduce_scatter | solution.py:173
  366.1 2.1 copy-start.5
  369.5 29.2 %reduce-scatter.3.cloned.1.call-start = ((), (), s32[]{:S(2)}) async-start(), calls=%async_computation.6 | async-start | bytes 4718592 | tf_op jit(solution)/shard_map/reduce_scatter | solution.py:176
  383.7 17.8 %copy-start.13 = (f32[8,32,64]{2,1,0:T(8,128)S(1)}, f32[8,32,64]{2,1,0:T(8,128)}, u32[]{:S(2)}) copy-start(f32[8,32,64]{2,1,0:T(8,128)} %param.16) | copy-start | bytes 196612
  400.8 2.1 copy-start.4
Sparse Core Ops, SparseCore 0:
  12.8 16.1 all-gather.5
  31.2 16.1 all-gather.7
  70.0 123.0 all-gather.9
  195.0 121.7 all-gather.11
  369.6 11.7 reduce-scatter.4
  383.7 14.9 reduce-scatter.2
where the time goes:
time: 412 us; the launch traced here: 410 us
  waiting for transfers between devices  218 us (53%)
  local copies, waits for them, and re-layouts  82.8 us (20%)
  matrix products  57.6 us (14%)
  other arithmetic  33.3 us (8%)
  between operations  14.4 us (3%)
    all_gather x1, waiting for transfers between devices, per_device(): lax.all_gather(keys, 'row', axis=1, tiled=True)  115 us
    all_gather x1, waiting for transfers between devices, per_device(): lax.all_gather(values, 'row', axis=1, tiled=True)  70.3 us
    all_gather x1, local copies, waits for them, and re-layouts, per_device(): lax.all_gather(keys, 'row', axis=1, tiled=True)  24.9 us
    all_gather x1, local copies, waits for them, and re-layouts, per_device(): lax.all_gather(values, 'row', axis=1, tiled=True)  24.7 us
    unnamed x30, local copies, waits for them, and re-layouts  20.9 us
    dot_general x1, matrix products, absorb(): jnp.einsum('shqk,skhd->shqd', weights.astype(jnp.bfloat16), value_split,...  18.1 us
    dot_general x1, matrix products, absorb(): jnp.einsum('sqhd,skhd->shqk', query, key_split, preferred_element_type=jn...  16.8 us
    reduce_scatter x1, waiting for transfers between devices, per_device(): lax.psum_scatter(partial_sum[:, text_rows:].astype(jnp.bfloat16), 'col',...  15 us
  transfers between devices with their start and end apart: 6, of which 5 were waited for; matrix products, arithmetic and copies ran while one was open for 22% of the time, Pallas kernels for 0%

commit v1 on v0

--- a/solution.py
+++ b/solution.py
@@ -158,7 +158,9 @@
     )
     piece = (
         lax.all_gather(keys, "row", axis=1, tiled=True),
-        lax.all_gather(values, "row", axis=1, tiled=True),
+        jnp.concatenate(
+            lax.all_to_all(jnp.stack([values] * lax.axis_size("row")), "row", 0, 0), axis=1
+        ),
     )
     count = piece[0].shape[1]
     valid = valid_keys(text_len, block_keep, count, text_rows, img_rows)

time: 412 us -> 629 us (1.53)
  waiting for transfers between devices: 218 us -> 393 us
  local copies, waits for them, and re-layouts: 82.8 us -> 119 us
  starting transfers between devices: 0.65 us -> 7.29 us
    all_to_all x0 -> x1, waiting for transfers between devices: none -> 335 us  [per_device(): lax.all_to_all(jnp.stack([values] * lax.axis_size('row')), 'row', 0, 0)]
    all_gather x1, waiting for transfers between devices: 115 us -> 0.01 us  [per_device(): lax.all_gather(keys, 'row', axis=1, tiled=True)]
    all_gather x1 -> x0, waiting for transfers between devices: 70.3 us -> none  [per_device(): lax.all_gather(values, 'row', axis=1, tiled=True)]
    another operation x0 -> x2, local copies, waits for them, and re-layouts: none -> 47 us  [the longest x1 38.6 us: absorb(): value_split = value_piece.reshape(samples, count, heads, head_dim)]
    reduce_scatter x1, waiting for transfers between devices: 7.85 us -> 33.3 us  [per_device(): lax.psum_scatter(partial_sum[:, :text_rows].astype(jnp.bfloat16), 'col',...]
    all_gather x1 -> x0, local copies, waits for them, and re-layouts: 24.7 us -> none  [per_device(): lax.all_gather(values, 'row', axis=1, tiled=True)]
    reshape x0 -> x1, local copies, waits for them, and re-layouts: none -> 17.1 us  [per_device(): jnp.concatenate(lax.all_to_all(jnp.stack([values] * lax.axis_size('row'))...]
    all_to_all x0 -> x1, starting transfers between devices: none -> 6.91 us  [per_device(): lax.all_to_all(jnp.stack([values] * lax.axis_size('row')), 'row', 0, 0)]
  transfers between devices with their start and end apart: 6 -> 6, of which waited for: 5 -> 4; matrix products, arithmetic and copies ran while one was open for 22% -> 15% of each run, Pallas kernels for 0% -> 0%
where the time goes in v1:
time: 629 us; the launch traced here: 626 us
  waiting for transfers between devices  393 us (62%)
  local copies, waits for them, and re-layouts  119 us (19%)
  matrix products  57.2 us (9%)
  other arithmetic  32.3 us (5%)
  between operations  14.1 us (2%)
  starting transfers between devices  7.29 us (1%)
    all_to_all x1, waiting for transfers between devices, per_device(): lax.all_to_all(jnp.stack([values] * lax.axis_size('row')), 'row', 0, 0)  335 us
    another operation x1, local copies, waits for them, and re-layouts, absorb(): value_split = value_piece.reshape(samples, count, heads, head_dim)  38.6 us
    reduce_scatter x1, waiting for transfers between devices, per_device(): lax.psum_scatter(partial_sum[:, :text_rows].astype(jnp.bfloat16), 'col',...  33.3 us
    all_gather x1, local copies, waits for them, and re-layouts, per_device(): lax.all_gather(keys, 'row', axis=1, tiled=True)  24.8 us
    unnamed x42, local copies, waits for them, and re-layouts  21 us
    dot_general x1, matrix products, absorb(): jnp.einsum('shqk,skhd->shqd', weights.astype(jnp.bfloat16), value_split,...  19.1 us
    reshape x1, local copies, waits for them, and re-layouts, per_device(): jnp.concatenate(lax.all_to_all(jnp.stack([values] * lax.axis_size('row'))...  17.1 us
    dot_general x1, matrix products, absorb(): jnp.einsum('sqhd,skhd->shqk', query, key_split, preferred_element_type=jn...  15.3 us
  transfers between devices with their start and end apart: 6, of which 4 were waited for; matrix products, arithmetic and copies ran while one was open for 15% of the time, Pallas kernels for 0%

profile of v1, /device:TPU:1, one launch (start us, length us, event | category | flops | bytes accessed | tf_op | source)
XLA Modules:
  0.0 626.2 jit_solution(9242016070013237366)
XLA Ops:
  14.3 2.0 fusion.21
  16.3 2.9 all-gather
  19.3 18.7 %copy.37 = bf16[3072,3,768]{0,2,1:T(8,128)(2,1)} copy(bf16[3072,3,768]{2,0,1:T(8,128)(2,1)} %param.22) | data formatting | bytes 28311552 | tf_op args[8]
  38.5 9.6 %all-gather.7.cloned.1.call-done = bf16[8,64,3072]{2,1,0:T(8,128)(2,1)} async-done(((bf16[8,32,3072]{2,1,0:T(8,128)(2,1)}), bf16[8,64,3072]{2,1,0:T(8,128)(2,1)}) %all-gather.7.cloned.1.call-update) | async-done | bytes 3145744 | tf_op jit(solution)/shard_map/all_gather | solution.py:130
  48.1 14.8 %fusion.10 = f32[8,96,3,6,128]{4,1,3,2,0:T(8,128)S(1)} fusion(bf16[3,6,128,3072,1]{3,2,1,0,4:T(8,128)(2,1)} %bitcast.90, bf16[8,64,3072]{2,1,0:T(8,128)(2,1)} %all-gather.7.cloned.1.call-done, bf16[8,32,3072]{2,1,0:T(8,128)(2,1)} %all-gather.5.cloned.1.call-done), kind=kOutput, calls=%fused_computation.16 | convolution fusion | flops 10881073152 | bytes 25952256 | tf_op jit(solution)/shard_map/dot_general | solution.py:137
  66.2 2.5 subtract_convert_fusion.1
  70.4 1.8 slice.129
  72.7 2.2 convert_element_type.71
  74.9 8.4 %stack.3 = bf16[16,8,96,768]{3,2,1,0:T(8,128)(2,1)} broadcast(bf16[8,96,768]{2,1,0:T(8,128)(2,1)} %convert_element_type.71), dimensions={1,2,3} | broadcast | bytes 20054016 | tf_op jit(solution)/shard_map/stack | solution.py:162
  83.4 6.9 %all-to-all-start = ((bf16[16,8,96,768]{3,2,1,0:T(8,128)(2,1)}), bf16[16,8,96,768]{3,2,1,0:T(8,128)(2,1)}, u32[]{:S(2)}, u32[]{:S(2)}) async-start(bf16[16,8,96,768]{3,2,1,0:T(8,128)(2,1)} %stack.3), calls=%async_computation | async-start | bytes 37748736 | tf_op jit(solution)/shard_map/all_to_all | solution.py:162
  90.9 334.9 %all-to-all-done = bf16[16,8,96,768]{3,2,1,0:T(8,128)(2,1)} async-done(((bf16[16,8,96,768]{3,2,1,0:T(8,128)(2,1)}), bf16[16,8,96,768]{3,2,1,0:T(8,128)(2,1)}, u32[]{:S(2)}, u32[]{:S(2)}) %all-to-all-start) | async-done | bytes 18874400 | tf_op jit(solution)/shard_map/all_to_all | solution.py:162
  425.8 17.1 %copy.44 = bf16[8,16,96,768]{3,2,1,0:T(8,128)(2,1)} copy(bf16[8,16,96,768]{3,2,0,1:T(8,128)(2,1)} %bitcast.20) | data formatting | bytes 37748736 | tf_op jit(solution)/shard_map/reshape | solution.py:161
  443.0 38.6 %reshape_reshape.4 = bf16[8,1536,6,128]{3,2,1,0:T(8,128)(2,1)} reshape(bf16[8,16,96,768]{3,2,1,0:T(8,128)(2,1)} %copy.44) | data formatting | bytes 37748736 | tf_op jit(solution)/shard_map/reshape;reshape | solution.py:89
  481.6 24.8 %copy.41 = bf16[8,1536,768]{1,2,0:T(8,128)(2,1)} copy(bf16[8,1536,768]{2,1,0:T(8,128)(2,1)} %all-gather.9.cloned.1.call-done) | data formatting | bytes 37748736 | tf_op jit(solution)/shard_map/all_gather | solution.py:160
  506.3 15.3 %fusion = (f32[8,6,96]{2,1,0:T(8,128)S(1)}, f32[8,6,96,1536]{3,2,1,0:T(8,128)}) fusion(pred[8,1536]{1,0:T(8,128)(4,1)S(1)} %compare_select_fusion, bf16[8,1536,6,128]{1,3,2,0:T(8,128)(2,1)} %bitcast.89, bf16[8,96,6,64]{3,1,2,0:T(8,128)(2,1)S(1)} %copy-done.7, bf16[8,96,6,64]{3,1,2,0:T(8,128)(2,1)S(1)} %get-tuple-element.9), kind=kOutput, calls=%fused_computation.2 | convolution fusion | flops 1835527680 | bytes 48396288 | tf_op jit(solution)/shard_map/sqhd,skhd->shqk/dot_general | solution.py:90
  521.7 10.2 %fusion.1 = f32[8,6,96]{2,1,0:T(8,128)S(1)} fusion(f32[8,6,96,1536]{3,2,1,0:T(8,128)} %get-tuple-element.30, f32[8,6,96]{2,1,0:T(8,128)S(1)} %get-tuple-element.21, pred[8,1536]{1,0:T(8,128)(4,1)S(1)} %compare_select_fusion), kind=kLoop, calls=%fused_computation.3 | loop fusion | flops 28306944 | bytes 28360704 | tf_op jit(solution)/shard_map/reduce_sum | solution.py:97
  531.9 19.1 %fusion.42 = bf16[8,6,12,8,128]{4,3,2,1,0:T(8,128)(2,1)S(1)} fusion(bf16[8,1536,6,128]{3,2,1,0:T(8,128)(2,1)} %reshape_reshape.4, f32[8,6,96,1536]{3,2,1,0:T(8,128)} %get-tuple-element.30, f32[8,6,96]{2,1,0:T(8,128)S(1)} %get-tuple-element.21, pred[8,1536]{1,0:T(8,128)(4,1)S(1)} %compare_select_fusion, f32[8,96,6]{1,2,0:T(8,128)S(1)} %bitcast_add_fusion.1, ...), kind=kOutput, calls=%fused_computation.60 | convolution fusion | flops 1842020352 | bytes 48433152 | tf_op jit(solution)/shard_map/shqk,skhd->shqd/dot_general | solution.py:98
  551.1 6.5 %convolution_convert_fusion = bf16[8,96,3072]{2,1,0:T(8,128)(2,1)S(1)} fusion(bf16[768,3072]{1,0:T(8,128)(2,1)} %param.23, bf16[8,6,12,8,128]{4,3,2,1,0:T(8,128)(2,1)S(1)} %fusion.42), kind=kOutput, calls=%fused_computation.11 | convolution fusion | flops 3626237952 | bytes 10616832 | tf_op jit(solution)/shard_map/dot_general | solution.py:170
  557.6 2.1 copy-done.8
  561.0 3.7 slice.92
  564.8 33.3 %reduce-scatter.5.cloned.1.call-done = bf16[8,16,3072]{2,1,0:T(8,128)(2,1)} async-done(((bf16[8,32,3072]{2,1,0:T(8,128)(2,1)}), bf16[8,16,3072]{2,1,0:T(8,128)(2,1)}) %reduce-scatter.5.cloned.1.call-update) | async-done | bytes 786448 | tf_op jit(solution)/shard_map/reduce_scatter | solution.py:175
  598.1 2.3 fusion.39
  600.4 15.0 %reduce-scatter.3.cloned.1.call-done = bf16[8,32,3072]{2,1,0:T(8,128)(2,1)} async-done(((bf16[8,64,3072]{2,1,0:T(8,128)(2,1)}), bf16[8,32,3072]{2,1,0:T(8,128)(2,1)}) %reduce-scatter.3.cloned.1.call-update) | async-done | bytes 1572880 | tf_op jit(solution)/shard_map/reduce_scatter | solution.py:178
  615.4 2.1 convert_reduce_fusion.1
  (86 shorter events, 17.0 us)
Async XLA Ops:
  7.2 611.0 %copy-start = (bf16[3072,64]{0,1:T(8,128)(2,1)S(1)}, bf16[3072,64]{0,1:T(8,128)(2,1)}, u32[]{:S(2)}) copy-start(bf16[3072,64]{0,1:T(8,128)(2,1)} %param.24) | copy-start | bytes 1179652
  7.2 4.9 copy-start.4
  7.2 31.3 %all-gather.5.cloned.1.call-start = ((), (), s32[]{:S(2)}) async-start(), calls=%async_computation.3 | async-start | bytes 2359296 | tf_op jit(solution)/shard_map/all_gather | solution.py:129
  8.6 4.8 copy-start.1
  13.4 34.7 %all-gather.7.cloned.1.call-start = ((), (), s32[]{:S(2)}) async-start(), calls=%async_computation.4 | async-start | bytes 4718592 | tf_op jit(solution)/shard_map/all_gather | solution.py:130
  16.3 465.3 %all-gather.9.cloned.1.call-start = ((), (), s32[]{:S(2)}) async-start(), calls=%async_computation.5 | async-start | bytes 20054016 | tf_op jit(solution)/shard_map/all_gather | solution.py:160
  19.3 18.8 %copy-start.14 = (f32[2,128]{1,0:T(2,128)S(1)}, f32[2,128]{1,0:T(2,128)}, u32[]{:S(2)}) copy-start(f32[2,128]{1,0:T(2,128)} %param.21) | copy-start | bytes 3076
  19.3 18.8 %copy-start.16 = (f32[64]{0:T(128)S(1)}, f32[64]{0:T(128)}, u32[]{:S(2)}) copy-start(f32[64]{0:T(128)} %constant.82.clone) | copy-start | bytes 772
  19.3 18.8 %copy-start.17 = (f32[64]{0:T(128)S(1)}, f32[64]{0:T(128)}, u32[]{:S(2)}) copy-start(f32[64]{0:T(128)} %constant.81.clone) | copy-start | bytes 772
  19.3 18.8 %copy-start.18 = (f32[64]{0:T(128)S(1)}, f32[64]{0:T(128)}, u32[]{:S(2)}) copy-start(f32[64]{0:T(128)} %constant.80.clone) | copy-start | bytes 772
  62.9 3.3 copy-start.3
  83.4 7.2 %copy-start.12 = (s32[8,16]{1,0:T(8,128)S(1)}, s32[8,16]{1,0:T(8,128)}, u32[]{:S(2)}) copy-start(s32[8,16]{1,0:T(8,128)} %param.18) | copy-start | bytes 1540
  83.4 7.5 %copy-start.15 = (s32[8]{0:T(128)S(1)}, s32[8]{0:T(128)}, u32[]{:S(2)}) copy-start(s32[8]{0:T(128)} %param.17) | copy-start | bytes 100
  83.4 342.5 %all-to-all-start = ((bf16[16,8,96,768]{3,2,1,0:T(8,128)(2,1)}), bf16[16,8,96,768]{3,2,1,0:T(8,128)(2,1)}, u32[]{:S(2)}, u32[]{:S(2)}) async-start(bf16[16,8,96,768]{3,2,1,0:T(8,128)(2,1)} %stack.3), calls=%async_computation | async-start | bytes 37748736 | tf_op jit(solution)/shard_map/all_to_all | solution.py:162
  90.3 507.8 %reduce-scatter.5.cloned.1.call-start = ((), (), s32[]{:S(2)}) async-start(), calls=%async_computation.7 | async-start | bytes 2359296 | tf_op jit(solution)/shard_map/reduce_scatter | solution.py:175
  481.6 24.8 %copy-start.7 = (bf16[8,96,6,64]{3,1,2,0:T(8,128)(2,1)S(1)}, bf16[8,96,6,64]{3,1,2,0:T(8,128)(2,1)}, u32[]{:S(2)}) copy-start(bf16[8,96,6,64]{3,1,2,0:T(8,128)(2,1)} %get-tuple-element.10) | copy-start | bytes 1769476
  557.6 2.1 copy-start.8
  561.0 54.4 %reduce-scatter.3.cloned.1.call-start = ((), (), s32[]{:S(2)}) async-start(), calls=%async_computation.6 | async-start | bytes 4718592 | tf_op jit(solution)/shard_map/reduce_scatter | solution.py:178
  564.8 33.3 %copy-start.5 = (bf16[8,16,3072]{2,1,0:T(8,128)(2,1)S(1)}, bf16[8,16,3072]{2,1,0:T(8,128)(2,1)}, u32[]{:S(2)}) copy-start(bf16[8,16,3072]{2,1,0:T(8,128)(2,1)} %param.15) | copy-start | bytes 2359300
  564.8 33.3 %copy-start.9 = (f32[8,3072]{1,0:T(8,128)S(1)}, f32[8,3072]{1,0:T(8,128)}, u32[]{:S(2)}) copy-start(f32[8,3072]{1,0:T(8,128)} %get-tuple-element.17) | copy-start | bytes 294916
  564.8 50.6 %copy-start.2 = (bf16[8,32,3072]{2,1,0:T(8,128)(2,1)S(1)}, bf16[8,32,3072]{2,1,0:T(8,128)(2,1)}, u32[]{:S(2)}) copy-start(bf16[8,32,3072]{2,1,0:T(8,128)(2,1)} %param.14) | copy-start | bytes 4718596
  600.4 17.8 %copy-start.10 = (f32[8,3072]{1,0:T(8,128)S(1)}, f32[8,3072]{1,0:T(8,128)}, u32[]{:S(2)}) copy-start(f32[8,3072]{1,0:T(8,128)} %get-tuple-element.13) | copy-start | bytes 294916
  600.4 17.8 %copy-start.11 = (f32[8,3072]{1,0:T(8,128)S(1)}, f32[8,3072]{1,0:T(8,128)}, u32[]{:S(2)}) copy-start(f32[8,3072]{1,0:T(8,128)} %get-tuple-element.14) | copy-start | bytes 294916
  600.4 17.8 %copy-start.19 = (f32[8,32,64]{2,1,0:T(8,128)S(1)}, f32[8,32,64]{2,1,0:T(8,128)}, u32[]{:S(2)}) copy-start(f32[8,32,64]{2,1,0:T(8,128)} %param.16) | copy-start | bytes 196612
  (2 other events, 4.1 us)
Sparse Core Ops, SparseCore 0:
  13.5 16.1 all-gather.4
  31.9 16.1 all-gather.6
  70.5 377.1 all-gather.8
  561.1 36.9 reduce-scatter.4
  600.4 14.9 reduce-scatter.2
